TPU v7x, 512 devices: a whole 4x8x8 slice. The times are simulated.
512 devices in a mesh: head: 2 (over core), seq: 256 (over z, y, x).
Axes of the slice: x: 4, y: 8, z: 8, core: 2. Of those that a mesh axis runs over, the one named last changes fastest.
Arguments:
- query_matrix: bfloat16 [32, 32768, 128], P(None, ('seq', 'head')), may hold values from -6 to 6
- key_matrix: bfloat16 [8, 32768, 128], P(None, ('seq', 'head')), may hold values from -6 to 6
- value_matrix: bfloat16 [8, 32768, 128], P(None, ('seq', 'head')), may hold values from -6 to 6
- output_gradient: bfloat16 [32, 32768, 128], P(None, ('seq', 'head')), may hold values from -6 to 6
- query_head_spans: int32 [32], replicated, may hold values from 64 to 256, as said below
- slab_offset: int32 [1], replicated, may hold values from 0 to 8191
Outputs:
- attn_out: bfloat16 [32, 32768, 128], P(None, ('seq', 'head'))
- query_grad: bfloat16 [32, 32768, 128], P(None, ('seq', 'head'))
- key_grad: bfloat16 [8, 32768, 128], P(None, ('seq', 'head'))
- value_grad: bfloat16 [8, 32768, 128], P(None, ('seq', 'head'))
Inputs may be any that keep to these rules, and one draw needn't show every extreme that they name: `query_head_spans`: every span is a multiple of 64; some head has the span 4 * 64 and some head the span 64.
All inputs are finite; a program needn't handle non-finite values.
Results may differ from a plain program's by a relative error of at most 0.019.
Values may be sent and summed in bfloat16 or wider, within the bound.
A program may use at most 64 MiB of HBM per device.

v0:
```python
import jax
import jax.numpy as jnp
from jax import lax
from jax.sharding import PartitionSpec as P

REACH = 2
SEGMENT = 512


masked_score = -1e30


def shifted(block, axis, distance):
    devices = range(lax.axis_size(axis))
    route = [(i - distance, i) for i in devices if i - distance in devices]
    return lax.ppermute(block, axis, route)


def shards(query_matrix, key_matrix, value_matrix, output_gradient, query_head_spans, slab_offset):
    queries, keys_local, values_local, grads_in = (
        lax.all_to_all(query_matrix, "head", split_axis=0, concat_axis=1, tiled=True),
        lax.all_to_all(key_matrix, "head", split_axis=0, concat_axis=1, tiled=True),
        lax.all_to_all(value_matrix, "head", split_axis=0, concat_axis=1, tiled=True),
        lax.all_to_all(output_gradient, "head", split_axis=0, concat_axis=1, tiled=True),
    )
    heads_here = queries.shape[0]
    groups_here = keys_local.shape[0]
    heads_per_group = heads_here // groups_here
    block_length = queries.shape[1]
    head_size = queries.shape[2]
    score_scale = head_size ** (-0.5)
    head_index = lax.axis_index("head")
    seq_index = lax.axis_index("seq")
    span_per_row = lax.dynamic_slice_in_dim(
        query_head_spans, head_index * heads_here, heads_here
    ).reshape(groups_here, heads_per_group, 1, 1)
    doc_offset = slab_offset[0]
    query_grid = queries.reshape(groups_here, heads_per_group, block_length, head_size)
    grad_grid = grads_in.reshape(groups_here, heads_per_group, block_length, head_size)
    query_pos = seq_index * block_length + jnp.arange(block_length, dtype=jnp.int32)

    def visible_at(blocks_back):
        key_pos = (seq_index - blocks_back) * block_length + jnp.arange(
            block_length, dtype=jnp.int32
        )
        distance = query_pos[:, None] - key_pos[None, :]
        same_segment = (doc_offset + key_pos[None, :]) // SEGMENT == (
            doc_offset + query_pos[:, None]
        ) // SEGMENT
        inside = (distance >= 0) & (key_pos[None, :] >= 0) & same_segment
        return inside[None, None] & (distance[None, None] < span_per_row)

    def forward_step(online, key_block, value_block, blocks_back):
        visible = visible_at(blocks_back)

        def attend(carried):
            row_max, row_sum, weighted = carried
            scores = (
                jnp.einsum(
                    "gaqd,gkd->gaqk", query_grid, key_block, preferred_element_type=jnp.float32
                )
                * score_scale
            )
            new_max = jnp.maximum(
                row_max, jnp.max(jnp.where(visible, scores, masked_score), axis=-1, keepdims=True)
            )
            weights = jnp.where(visible, jnp.exp(scores - new_max), 0.0)
            factor = jnp.exp(row_max - new_max)
            row_sum = row_sum * factor + jnp.sum(weights, axis=-1, keepdims=True)
            weighted = weighted * factor + jnp.einsum(
                "gaqk,gkd->gaqd",
                weights.astype(jnp.bfloat16),
                value_block,
                preferred_element_type=jnp.float32,
            )
            return (new_max, row_sum, weighted)

        return lax.cond(jnp.any(visible), attend, lambda carried: carried, online)

    stat_shape = (groups_here, heads_per_group, block_length, 1)
    online = (
        jnp.full(stat_shape, masked_score, jnp.float32),
        jnp.zeros(stat_shape, jnp.float32),
        jnp.zeros(query_grid.shape, jnp.float32),
    )
    online = forward_step(online, keys_local, values_local, 0)
    window_keys = jnp.zeros((REACH + 1,) + keys_local.shape, keys_local.dtype).at[0].set(keys_local)
    window_values = (
        jnp.zeros((REACH + 1,) + values_local.shape, values_local.dtype).at[0].set(values_local)
    )

    def forward_hop(blocks_back, carried):
        moving, online, window_keys, window_values = carried
        moving = shifted((moving[0], moving[1]), "seq", 1)
        online = forward_step(online, moving[0], moving[1], blocks_back)
        window_keys = window_keys.at[blocks_back].set(moving[0])
        window_values = window_values.at[blocks_back].set(moving[1])
        return (moving, online, window_keys, window_values)

    finished = lax.fori_loop(
        1, REACH + 1, forward_hop, ((keys_local, values_local), online, window_keys, window_values)
    )
    online, window_keys, window_values = (finished[1], finished[2], finished[3])
    row_max, row_sum, weighted = online
    attn_grid = (weighted / row_sum).astype(jnp.bfloat16)
    log_total = row_max + jnp.log(row_sum)
    attn_out = lax.all_to_all(
        attn_grid.reshape(heads_here, block_length, head_size),
        "head",
        split_axis=1,
        concat_axis=0,
        tiled=True,
    )
    row_delta = jnp.sum(
        grad_grid.astype(jnp.float32) * attn_grid.astype(jnp.float32), axis=-1, keepdims=True
    )

    def backward_step(blocks_back, carried):
        visible = visible_at(blocks_back)
        key_block = window_keys[blocks_back]
        value_block = window_values[blocks_back]

        def differentiate(inner):
            query_acc, key_parts, value_parts = inner
            scores = (
                jnp.einsum(
                    "gaqd,gkd->gaqk", query_grid, key_block, preferred_element_type=jnp.float32
                )
                * score_scale
            )
            prob_rows = jnp.where(visible, jnp.exp(scores - log_total), 0.0)
            value_part = jnp.einsum(
                "gaqk,gaqd->gkd",
                prob_rows.astype(jnp.bfloat16),
                grad_grid,
                preferred_element_type=jnp.float32,
            )
            prob_grad = jnp.einsum(
                "gaqd,gkd->gaqk", grad_grid, value_block, preferred_element_type=jnp.float32
            )
            score_grad = (prob_rows * (prob_grad - row_delta) * score_scale).astype(jnp.bfloat16)
            query_acc = query_acc + jnp.einsum(
                "gaqk,gkd->gaqd", score_grad, key_block, preferred_element_type=jnp.float32
            )
            key_part = jnp.einsum(
                "gaqk,gaqd->gkd", score_grad, query_grid, preferred_element_type=jnp.float32
            )
            return (
                query_acc,
                key_parts.at[blocks_back].set(key_part),
                value_parts.at[blocks_back].set(value_part),
            )

        return lax.cond(jnp.any(visible), differentiate, lambda inner: inner, carried)

    part_shape = (REACH + 1, groups_here, block_length, head_size)
    query_acc, key_parts, value_parts = lax.fori_loop(
        0,
        REACH + 1,
        backward_step,
        (
            jnp.zeros(query_grid.shape, jnp.float32),
            jnp.zeros(part_shape, jnp.float32),
            jnp.zeros(part_shape, jnp.float32),
        ),
    )

    def collect(turn_idx, carried):
        blocks_back = REACH - 1 - turn_idx
        carried = (
            shifted(carried[0].astype(jnp.bfloat16), "seq", -1).astype(jnp.float32),
            shifted(carried[1].astype(jnp.bfloat16), "seq", -1).astype(jnp.float32),
        )
        return (carried[0] + key_parts[blocks_back], carried[1] + value_parts[blocks_back])

    key_total, value_total = lax.fori_loop(
        0, REACH, collect, (key_parts[REACH], value_parts[REACH])
    )
    query_grad, key_grad, value_grad = (
        lax.all_to_all(
            query_acc.reshape(heads_here, block_length, head_size).astype(jnp.bfloat16),
            "head",
            split_axis=1,
            concat_axis=0,
            tiled=True,
        ),
        lax.all_to_all(
            key_total.astype(jnp.bfloat16), "head", split_axis=1, concat_axis=0, tiled=True
        ),
        lax.all_to_all(
            value_total.astype(jnp.bfloat16), "head", split_axis=1, concat_axis=0, tiled=True
        ),
    )
    return (attn_out, query_grad, key_grad, value_grad)


def solution(mesh):
    return jax.shard_map(
        shards,
        mesh=mesh,
        in_specs=(
            P(None, ("seq", "head"), None),
            P(None, ("seq", "head"), None),
            P(None, ("seq", "head"), None),
            P(None, ("seq", "head"), None),
            P(),
            P(),
        ),
        out_specs=(
            P(None, ("seq", "head"), None),
            P(None, ("seq", "head"), None),
            P(None, ("seq", "head"), None),
            P(None, ("seq", "head"), None),
        ),
        check_vma=False,
    )
```

profile of v0, /device:TPU:255, one launch (start us, length us, event | category | flops | bytes accessed | tf_op | source)
XLA Modules:
  0.0 147.7 jit_solution(13357513403248189156)
XLA Ops:
  0.6 4.2 %all-to-all-start.2 = ((bf16[32,64,128]{2,1,0:T(8,128)(2,1)}), bf16[32,64,128]{2,1,0:T(8,128)(2,1)S(1)}, u32[]{:S(2)}, u32[]{:S(2)}) async-start(bf16[32,64,128]{2,1,0:T(8,128)(2,1)} %param.30), calls=%async_computation.2 | async-start | bytes 1048576 | tf_op jit(solution)/shard_map/all_to_all | solution.py:21
  7.1 3.4 %all-to-all-start = ((bf16[8,64,128]{2,1,0:T(8,128)(2,1)}), bf16[8,64,128]{2,1,0:T(8,128)(2,1)S(1)}, u32[]{:S(2)}, u32[]{:S(2)}) async-start(bf16[8,64,128]{2,1,0:T(8,128)(2,1)} %param.31), calls=%async_computation | async-start | bytes 262144 | tf_op jit(solution)/shard_map/all_to_all | solution.py:22
  11.6 3.7 %all-to-all-start.1 = ((bf16[8,64,128]{2,1,0:T(8,128)(2,1)}), bf16[8,64,128]{2,1,0:T(8,128)(2,1)S(1)}, u32[]{:S(2)}, u32[]{:S(2)}) async-start(bf16[8,64,128]{2,1,0:T(8,128)(2,1)} %param.32), calls=%async_computation.1 | async-start | bytes 262144 | tf_op jit(solution)/shard_map/all_to_all | solution.py:23
  16.4 3.8 %all-to-all-start.4 = ((bf16[32,64,128]{2,1,0:T(8,128)(2,1)}), bf16[32,64,128]{2,1,0:T(8,128)(2,1)S(1)}, u32[]{:S(2)}, u32[]{:S(2)}) async-start(bf16[32,64,128]{2,1,0:T(8,128)(2,1)} %param.33), calls=%async_computation.4 | async-start | bytes 1048576 | tf_op jit(solution)/shard_map/all_to_all | solution.py:24
  23.1 2.3 %conditional.3 = (f32[4,4,128,1]{2,1,0,3:T(4,128)S(1)}, f32[4,4,128,1]{2,1,0,3:T(4,128)S(1)}, f32[4,4,128,128]{3,2,1,0:T(8,128)S(1)}) conditional(s32[]{:T(128)} %convert_element_type.106, () %tuple.149, (bf16[4,4,128,128]{3,2,1,0:T(8,128)(2,1)S(1)}, bf16[4,128,128]{2,1,0:T(8,128)(2,1)}, pred[4,4,128,128]{2,3,1,0:T(32,128)(4,1)S(1)}, ...), branch_computations={%region_1.2_spmd, %region_2.5_spmd} | conditional | flops 136849408 | bytes 5865496 | solution.py:78
  25.4 31.7 %while.75 = (s32[]{:T(128)}, bf16[4,128,128]{2,1,0:T(8,128)(2,1)}, bf16[4,128,128]{2,1,0:T(8,128)(2,1)S(1)}, f32[4,4,128,1]{2,1,0,3:T(4,128)S(1)}, f32[4,4,128,1...) while((s32[]{:T(128)}, bf16[4,128,128]{2,1,0:T(8,128)(2,1)}, ...), condition=%wide.region_12.13_spmd.clone, body=%wide.region_5.12_spmd.clone.sunk | while | flops 138128160 | bytes 9738124 | solution.py:100
  25.4 4.3 %collective-permute-start.2 = (bf16[4,128,128]{2,1,0:T(8,128)(2,1)}, bf16[4,128,128]{2,1,0:T(8,128)(2,1)S(1)}, u32[]{:S(2)}, u32[]{:S(2)}) collective-permute-start(bf16[4,128,128]{2,1,0:T(8,128)(2,1)} %get-tuple-element.1681), channel_id=1, source_target_pairs={{0,1},{1,2},{2,3},{3,4},{4,5},{5,6},{6,7},{7,8},{8,9},{9,10},{10,1... | collective-permute-start | bytes 393224 | tf_op jit(solution)/shard_map/while/body/eval_jaxpr/ppermute | solution.py:16
  29.8 3.1 %collective-permute-start.3 = (bf16[4,128,128]{2,1,0:T(8,128)(2,1)S(1)}, bf16[4,128,128]{2,1,0:T(8,128)(2,1)S(1)}, u32[]{:S(2)}, u32[]{:S(2)}) collective-permute-start(bf16[4,128,128]{2,1,0:T(8,128)(2,1)S(1)} %get-tuple-element.1682), channel_id=1, source_target_pairs={{0,1},{1,2},{2,3},{3,4},{4,5},{5,6},{6,7},{7,8},{8,9},{9,10},{10,1... | collective-permute-start | bytes 393224 | tf_op jit(solution)/shard_map/while/body/eval_jaxpr/ppermute | solution.py:16
  33.8 1.7 %fusion.62 = (pred[]{:T(512)}, pred[4,4,128,128]{2,3,1,0:T(32,128)(4,1)S(1)}) fusion(s32[4,4]{1,0:T(4,128)} %bitcast.164, s32[128,128]{0,1:T(8,128)S(1)} %broadcast_subtract_fusion.5, pred[128,128]{0,1:T(8,128)(4,1)S(1)} %compare_and_fusion.11), kind=kLoop, calls=%fused_computation.111.clone.1 | loop fusion | flops 786431 | bytes 344129 | tf_op jit(solution)/shard_map/while/body/eval_jaxpr/reduce_or | solution.py:78
  37.6 1.5 conditional.8
  41.1 7.4 %collective-permute-start.2 = (bf16[4,128,128]{2,1,0:T(8,128)(2,1)}, bf16[4,128,128]{2,1,0:T(8,128)(2,1)S(1)}, u32[]{:S(2)}, u32[]{:S(2)}) collective-permute-start(bf16[4,128,128]{2,1,0:T(8,128)(2,1)} %get-tuple-element.1681), channel_id=1, source_target_pairs={{0,1},{1,2},{2,3},{3,4},{4,5},{5,6},{6,7},{7,8},{8,9},{9,10},{10,1... | collective-permute-start | bytes 393224 | tf_op jit(solution)/shard_map/while/body/eval_jaxpr/ppermute | solution.py:16
  48.5 1.9 %collective-permute-start.3 = (bf16[4,128,128]{2,1,0:T(8,128)(2,1)S(1)}, bf16[4,128,128]{2,1,0:T(8,128)(2,1)S(1)}, u32[]{:S(2)}, u32[]{:S(2)}) collective-permute-start(bf16[4,128,128]{2,1,0:T(8,128)(2,1)S(1)} %get-tuple-element.1682), channel_id=1, source_target_pairs={{0,1},{1,2},{2,3},{3,4},{4,5},{5,6},{6,7},{7,8},{8,9},{9,10},{10,1... | collective-permute-start | bytes 393224 | tf_op jit(solution)/shard_map/while/body/eval_jaxpr/ppermute | solution.py:16
  51.3 1.7 %fusion.62 = (pred[]{:T(512)}, pred[4,4,128,128]{2,3,1,0:T(32,128)(4,1)S(1)}) fusion(s32[4,4]{1,0:T(4,128)} %bitcast.164, s32[128,128]{0,1:T(8,128)S(1)} %broadcast_subtract_fusion.5, pred[128,128]{0,1:T(8,128)(4,1)S(1)} %compare_and_fusion.11), kind=kLoop, calls=%fused_computation.111.clone.1 | loop fusion | flops 786431 | bytes 344129 | tf_op jit(solution)/shard_map/while/body/eval_jaxpr/reduce_or | solution.py:78
  60.3 22.4 %while.76 = (s32[]{:T(128)}, f32[4,4,128,128]{3,2,1,0:T(8,128)S(1)}, f32[3,4,128,128]{3,2,1,0:T(8,128)S(1)}, f32[3,4,128,128]{3,2,1,0:T(8,128)}, s32[]{:T(128)},...) while((s32[]{:T(128)}, ...), condition=%wide.region_19.20_spmd.clone, body=%wide.region_14.0_spmd.clone.sunk | while | flops 338924320 | bytes 17357180 | solution.py:157
  61.2 1.7 %fusion.65 = (pred[]{:T(512)}, pred[4,4,128,128]{2,3,1,0:T(32,128)(4,1)S(1)}) fusion(s32[4,4]{1,0:T(4,128)} %bitcast.166, s32[128,128]{0,1:T(8,128)S(1)} %broadcast_subtract_fusion.6, pred[128,128]{0,1:T(8,128)(4,1)S(1)} %compare_and_fusion.12), kind=kLoop, calls=%fused_computation.112.clone.1 | loop fusion | flops 786431 | bytes 344129 | tf_op jit(solution)/shard_map/while/body/eval_jaxpr/reduce_or | solution.py:154
  63.5 6.4 %conditional.9 = ((f32[4,4,128,128]{3,2,1,0:T(8,128)S(1)}, f32[3,4,128,128]{3,2,1,0:T(8,128)S(1)}, f32[3,4,128,128]{3,2,1,0:T(8,128)})) conditional(s32[]{:T(128)} %convert_element_type.138, (f32[4,4,128,128]{3,2,1,0:T(8,128)S(1)}, f32[3,4,128,128]{3,2,1,0:T(8,128)S(1)}, f32[3,4,128,128]{3,2,1,0:T(8,128)}) %tuple.218, (s32[]{:T(128)}, ...), branch_computations={%region_16.16_spmd, %region_17.18_spmd} | conditional | flops 338034720 | bytes 16925440 | solution.py:154
  70.8 1.7 %fusion.65 = (pred[]{:T(512)}, pred[4,4,128,128]{2,3,1,0:T(32,128)(4,1)S(1)}) fusion(s32[4,4]{1,0:T(4,128)} %bitcast.166, s32[128,128]{0,1:T(8,128)S(1)} %broadcast_subtract_fusion.6, pred[128,128]{0,1:T(8,128)(4,1)S(1)} %compare_and_fusion.12), kind=kLoop, calls=%fused_computation.112.clone.1 | loop fusion | flops 786431 | bytes 344129 | tf_op jit(solution)/shard_map/while/body/eval_jaxpr/reduce_or | solution.py:154
  73.1 6.4 %conditional.9 = ((f32[4,4,128,128]{3,2,1,0:T(8,128)S(1)}, f32[3,4,128,128]{3,2,1,0:T(8,128)S(1)}, f32[3,4,128,128]{3,2,1,0:T(8,128)})) conditional(s32[]{:T(128)} %convert_element_type.138, (f32[4,4,128,128]{3,2,1,0:T(8,128)S(1)}, f32[3,4,128,128]{3,2,1,0:T(8,128)S(1)}, f32[3,4,128,128]{3,2,1,0:T(8,128)}) %tuple.218, (s32[]{:T(128)}, ...), branch_computations={%region_16.16_spmd, %region_17.18_spmd} | conditional | flops 338034720 | bytes 16925440 | solution.py:154
  80.4 1.7 %fusion.65 = (pred[]{:T(512)}, pred[4,4,128,128]{2,3,1,0:T(32,128)(4,1)S(1)}) fusion(s32[4,4]{1,0:T(4,128)} %bitcast.166, s32[128,128]{0,1:T(8,128)S(1)} %broadcast_subtract_fusion.6, pred[128,128]{0,1:T(8,128)(4,1)S(1)} %compare_and_fusion.12), kind=kLoop, calls=%fused_computation.112.clone.1 | loop fusion | flops 786431 | bytes 344129 | tf_op jit(solution)/shard_map/while/body/eval_jaxpr/reduce_or | solution.py:154
  83.7 37.4 %while.74 = (s32[]{:T(128)}, bf16[4,128,128]{2,1,0:T(8,128)(2,1)S(1)}, bf16[4,128,128]{2,1,0:T(8,128)(2,1)S(1)}, f32[3,4,128,128]{3,2,1,0:T(8,128)S(1)}, f32[3,4...) while((s32[]{:T(128)}, bf16[4,128,128]{2,1,0:T(8,128)(2,1)S(1)}, ...), condition=%wide.region_21.22_spmd, body=%wide.region_20.21_spmd.sunk | while | flops 393222 | bytes 2097379 | solution.py:176
  83.7 11.2 %collective-permute-start = (bf16[4,128,128]{2,1,0:T(8,128)(2,1)S(1)}, bf16[4,128,128]{2,1,0:T(8,128)(2,1)S(1)}, u32[]{:S(2)}, u32[]{:S(2)}) collective-permute-start(bf16[4,128,128]{2,1,0:T(8,128)(2,1)S(1)} %get-tuple-element.1775), channel_id=1, source_target_pairs={{1,0},{2,1},{3,2},{4,3},{5,4},{6,5},{7,6},{8,7},{9,8},{10,9},{11,1... | collective-permute-start | bytes 393224 | tf_op jit(solution)/shard_map/while/body/eval_jaxpr/ppermute | solution.py:16
  94.9 1.9 %collective-permute-start.1 = (bf16[4,128,128]{2,1,0:T(8,128)(2,1)S(1)}, bf16[4,128,128]{2,1,0:T(8,128)(2,1)S(1)}, u32[]{:S(2)}, u32[]{:S(2)}) collective-permute-start(bf16[4,128,128]{2,1,0:T(8,128)(2,1)S(1)} %get-tuple-element.1776), channel_id=1, source_target_pairs={{1,0},{2,1},{3,2},{4,3},{5,4},{6,5},{7,6},{8,7},{9,8},{10,9},{11,1... | collective-permute-start | bytes 393224 | tf_op jit(solution)/shard_map/while/body/eval_jaxpr/ppermute | solution.py:16
  96.8 5.2 %collective-permute-done = bf16[4,128,128]{2,1,0:T(8,128)(2,1)S(1)} collective-permute-done((bf16[4,128,128]{2,1,0:T(8,128)(2,1)S(1)}, bf16[4,128,128]{2,1,0:T(8,128)(2,1)S(1)}, u32[]{:S(2)}, u32[]{:S(2)}) %collective-permute-start) | collective-permute-done | bytes 131104 | tf_op jit(solution)/shard_map/while/body/eval_jaxpr/ppermute | solution.py:16
  102.1 4.0 %collective-permute-done.1 = bf16[4,128,128]{2,1,0:T(8,128)(2,1)S(1)} collective-permute-done((bf16[4,128,128]{2,1,0:T(8,128)(2,1)S(1)}, bf16[4,128,128]{2,1,0:T(8,128)(2,1)S(1)}, u32[]{:S(2)}, u32[]{:S(2)}) %collective-permute-start.1) | collective-permute-done | bytes 131104 | tf_op jit(solution)/shard_map/while/body/eval_jaxpr/ppermute | solution.py:16
  107.0 1.9 %collective-permute-start = (bf16[4,128,128]{2,1,0:T(8,128)(2,1)S(1)}, bf16[4,128,128]{2,1,0:T(8,128)(2,1)S(1)}, u32[]{:S(2)}, u32[]{:S(2)}) collective-permute-start(bf16[4,128,128]{2,1,0:T(8,128)(2,1)S(1)} %get-tuple-element.1775), channel_id=1, source_target_pairs={{1,0},{2,1},{3,2},{4,3},{5,4},{6,5},{7,6},{8,7},{9,8},{10,9},{11,1... | collective-permute-start | bytes 393224 | tf_op jit(solution)/shard_map/while/body/eval_jaxpr/ppermute | solution.py:16
  109.0 1.9 %collective-permute-start.1 = (bf16[4,128,128]{2,1,0:T(8,128)(2,1)S(1)}, bf16[4,128,128]{2,1,0:T(8,128)(2,1)S(1)}, u32[]{:S(2)}, u32[]{:S(2)}) collective-permute-start(bf16[4,128,128]{2,1,0:T(8,128)(2,1)S(1)} %get-tuple-element.1776), channel_id=1, source_target_pairs={{1,0},{2,1},{3,2},{4,3},{5,4},{6,5},{7,6},{8,7},{9,8},{10,9},{11,1... | collective-permute-start | bytes 393224 | tf_op jit(solution)/shard_map/while/body/eval_jaxpr/ppermute | solution.py:16
  110.9 7.3 %collective-permute-done = bf16[4,128,128]{2,1,0:T(8,128)(2,1)S(1)} collective-permute-done((bf16[4,128,128]{2,1,0:T(8,128)(2,1)S(1)}, bf16[4,128,128]{2,1,0:T(8,128)(2,1)S(1)}, u32[]{:S(2)}, u32[]{:S(2)}) %collective-permute-start) | collective-permute-done | bytes 131104 | tf_op jit(solution)/shard_map/while/body/eval_jaxpr/ppermute | solution.py:16
  118.2 1.9 %collective-permute-done.1 = bf16[4,128,128]{2,1,0:T(8,128)(2,1)S(1)} collective-permute-done((bf16[4,128,128]{2,1,0:T(8,128)(2,1)S(1)}, bf16[4,128,128]{2,1,0:T(8,128)(2,1)S(1)}, u32[]{:S(2)}, u32[]{:S(2)}) %collective-permute-start.1) | collective-permute-done | bytes 131104 | tf_op jit(solution)/shard_map/while/body/eval_jaxpr/ppermute | solution.py:16
  121.9 7.7 %all-to-all-start.6 = ((bf16[4,128,128]{2,0,1:T(4,128)(2,1)}), bf16[4,128,128]{2,0,1:T(4,128)(2,1)S(1)}, u32[]{:S(2)}, u32[]{:S(2)}) async-start(bf16[4,128,128]{2,0,1:T(4,128)(2,1)} %copy.72), calls=%async_computation.6 | async-start | bytes 262144 | tf_op jit(solution)/shard_map/all_to_all | solution.py:187
  130.7 3.7 %all-to-all-start.7 = ((bf16[4,128,128]{2,0,1:T(4,128)(2,1)}), bf16[4,128,128]{2,0,1:T(4,128)(2,1)S(1)}, u32[]{:S(2)}, u32[]{:S(2)}) async-start(bf16[4,128,128]{2,0,1:T(4,128)(2,1)} %copy.71), calls=%async_computation.7 | async-start | bytes 262144 | tf_op jit(solution)/shard_map/all_to_all | solution.py:190
  136.4 3.6 %all-to-all-start.5 = ((bf16[16,128,128]{2,0,1:T(8,128)(2,1)}), bf16[16,128,128]{2,0,1:T(8,128)(2,1)S(1)}, u32[]{:S(2)}, u32[]{:S(2)}) async-start(bf16[16,128,128]{2,0,1:T(8,128)(2,1)} %bitcast.59), calls=%async_computation.5 | async-start | bytes 1048576 | tf_op jit(solution)/shard_map/all_to_all | solution.py:180
  141.9 3.5 %all-to-all-start.3 = ((bf16[16,128,128]{2,0,1:T(8,128)(2,1)}), bf16[16,128,128]{2,0,1:T(8,128)(2,1)S(1)}, u32[]{:S(2)}, u32[]{:S(2)}) async-start(bf16[16,128,128]{2,0,1:T(8,128)(2,1)} %bitcast.48), calls=%async_computation.3 | async-start | bytes 1048576 | tf_op jit(solution)/shard_map/all_to_all | solution.py:107
  (132 shorter events, 47.7 us)
Async XLA Ops:
  0.6 6.4 %all-to-all-start.2 = ((bf16[32,64,128]{2,1,0:T(8,128)(2,1)}), bf16[32,64,128]{2,1,0:T(8,128)(2,1)S(1)}, u32[]{:S(2)}, u32[]{:S(2)}) async-start(bf16[32,64,128]{2,1,0:T(8,128)(2,1)} %param.30), calls=%async_computation.2 | async-start | bytes 1048576 | tf_op jit(solution)/shard_map/all_to_all | solution.py:21
  4.8 0.7 copy-start.7
  7.1 4.5 %all-to-all-start = ((bf16[8,64,128]{2,1,0:T(8,128)(2,1)}), bf16[8,64,128]{2,1,0:T(8,128)(2,1)S(1)}, u32[]{:S(2)}, u32[]{:S(2)}) async-start(bf16[8,64,128]{2,1,0:T(8,128)(2,1)} %param.31), calls=%async_computation | async-start | bytes 262144 | tf_op jit(solution)/shard_map/all_to_all | solution.py:22
  11.6 4.8 %all-to-all-start.1 = ((bf16[8,64,128]{2,1,0:T(8,128)(2,1)}), bf16[8,64,128]{2,1,0:T(8,128)(2,1)S(1)}, u32[]{:S(2)}, u32[]{:S(2)}) async-start(bf16[8,64,128]{2,1,0:T(8,128)(2,1)} %param.32), calls=%async_computation.1 | async-start | bytes 262144 | tf_op jit(solution)/shard_map/all_to_all | solution.py:23
  16.4 6.6 %all-to-all-start.4 = ((bf16[32,64,128]{2,1,0:T(8,128)(2,1)}), bf16[32,64,128]{2,1,0:T(8,128)(2,1)S(1)}, u32[]{:S(2)}, u32[]{:S(2)}) async-start(bf16[32,64,128]{2,1,0:T(8,128)(2,1)} %param.33), calls=%async_computation.4 | async-start | bytes 1048576 | tf_op jit(solution)/shard_map/all_to_all | solution.py:24
  25.4 12.2 %collective-permute-start.2 = (bf16[4,128,128]{2,1,0:T(8,128)(2,1)}, bf16[4,128,128]{2,1,0:T(8,128)(2,1)S(1)}, u32[]{:S(2)}, u32[]{:S(2)}) collective-permute-start(bf16[4,128,128]{2,1,0:T(8,128)(2,1)} %get-tuple-element.1681), channel_id=1, source_target_pairs={{0,1},{1,2},{2,3},{3,4},{4,5},{5,6},{6,7},{7,8},{8,9},{9,10},{10,1... | collective-permute-start | bytes 393224 | tf_op jit(solution)/shard_map/while/body/eval_jaxpr/ppermute | solution.py:16
  29.8 7.8 %collective-permute-start.3 = (bf16[4,128,128]{2,1,0:T(8,128)(2,1)S(1)}, bf16[4,128,128]{2,1,0:T(8,128)(2,1)S(1)}, u32[]{:S(2)}, u32[]{:S(2)}) collective-permute-start(bf16[4,128,128]{2,1,0:T(8,128)(2,1)S(1)} %get-tuple-element.1682), channel_id=1, source_target_pairs={{0,1},{1,2},{2,3},{3,4},{4,5},{5,6},{6,7},{7,8},{8,9},{9,10},{10,1... | collective-permute-start | bytes 393224 | tf_op jit(solution)/shard_map/while/body/eval_jaxpr/ppermute | solution.py:16
  36.1 0.7 copy-start.5
  41.1 14.0 %collective-permute-start.2 = (bf16[4,128,128]{2,1,0:T(8,128)(2,1)}, bf16[4,128,128]{2,1,0:T(8,128)(2,1)S(1)}, u32[]{:S(2)}, u32[]{:S(2)}) collective-permute-start(bf16[4,128,128]{2,1,0:T(8,128)(2,1)} %get-tuple-element.1681), channel_id=1, source_target_pairs={{0,1},{1,2},{2,3},{3,4},{4,5},{5,6},{6,7},{7,8},{8,9},{9,10},{10,1... | collective-permute-start | bytes 393224 | tf_op jit(solution)/shard_map/while/body/eval_jaxpr/ppermute | solution.py:16
  48.5 6.6 %collective-permute-start.3 = (bf16[4,128,128]{2,1,0:T(8,128)(2,1)S(1)}, bf16[4,128,128]{2,1,0:T(8,128)(2,1)S(1)}, u32[]{:S(2)}, u32[]{:S(2)}) collective-permute-start(bf16[4,128,128]{2,1,0:T(8,128)(2,1)S(1)} %get-tuple-element.1682), channel_id=1, source_target_pairs={{0,1},{1,2},{2,3},{3,4},{4,5},{5,6},{6,7},{7,8},{8,9},{9,10},{10,1... | collective-permute-start | bytes 393224 | tf_op jit(solution)/shard_map/while/body/eval_jaxpr/ppermute | solution.py:16
  53.7 0.7 copy-start.5
  57.1 2.0 %copy-start.2 = (bf16[3,4,128,128]{3,2,1,0:T(8,128)(2,1)}, bf16[3,4,128,128]{3,2,1,0:T(8,128)(2,1)S(1)}, u32[]{:S(2)}) copy-start(bf16[3,4,128,128]{3,2,1,0:T(8,128)(2,1)S(1)} %get-tuple-element.1728) | copy-start | bytes 1179652
  59.3 1.0 copy-start.4
  65.7 0.7 copy-start.6
  67.0 1.1 copy-start
  69.0 0.9 copy-start.1
  75.2 0.7 copy-start.6
  76.6 1.1 copy-start
  78.6 0.9 copy-start.1
  83.7 18.3 %collective-permute-start = (bf16[4,128,128]{2,1,0:T(8,128)(2,1)S(1)}, bf16[4,128,128]{2,1,0:T(8,128)(2,1)S(1)}, u32[]{:S(2)}, u32[]{:S(2)}) collective-permute-start(bf16[4,128,128]{2,1,0:T(8,128)(2,1)S(1)} %get-tuple-element.1775), channel_id=1, source_target_pairs={{1,0},{2,1},{3,2},{4,3},{5,4},{6,5},{7,6},{8,7},{9,8},{10,9},{11,1... | collective-permute-start | bytes 393224 | tf_op jit(solution)/shard_map/while/body/eval_jaxpr/ppermute | solution.py:16
  94.9 11.1 %collective-permute-start.1 = (bf16[4,128,128]{2,1,0:T(8,128)(2,1)S(1)}, bf16[4,128,128]{2,1,0:T(8,128)(2,1)S(1)}, u32[]{:S(2)}, u32[]{:S(2)}) collective-permute-start(bf16[4,128,128]{2,1,0:T(8,128)(2,1)S(1)} %get-tuple-element.1776), channel_id=1, source_target_pairs={{1,0},{2,1},{3,2},{4,3},{5,4},{6,5},{7,6},{8,7},{9,8},{10,9},{11,1... | collective-permute-start | bytes 393224 | tf_op jit(solution)/shard_map/while/body/eval_jaxpr/ppermute | solution.py:16
  107.0 11.1 %collective-permute-start = (bf16[4,128,128]{2,1,0:T(8,128)(2,1)S(1)}, bf16[4,128,128]{2,1,0:T(8,128)(2,1)S(1)}, u32[]{:S(2)}, u32[]{:S(2)}) collective-permute-start(bf16[4,128,128]{2,1,0:T(8,128)(2,1)S(1)} %get-tuple-element.1775), channel_id=1, source_target_pairs={{1,0},{2,1},{3,2},{4,3},{5,4},{6,5},{7,6},{8,7},{9,8},{10,9},{11,1... | collective-permute-start | bytes 393224 | tf_op jit(solution)/shard_map/while/body/eval_jaxpr/ppermute | solution.py:16
  109.0 11.1 %collective-permute-start.1 = (bf16[4,128,128]{2,1,0:T(8,128)(2,1)S(1)}, bf16[4,128,128]{2,1,0:T(8,128)(2,1)S(1)}, u32[]{:S(2)}, u32[]{:S(2)}) collective-permute-start(bf16[4,128,128]{2,1,0:T(8,128)(2,1)S(1)} %get-tuple-element.1776), channel_id=1, source_target_pairs={{1,0},{2,1},{3,2},{4,3},{5,4},{6,5},{7,6},{8,7},{9,8},{10,9},{11,1... | collective-permute-start | bytes 393224 | tf_op jit(solution)/shard_map/while/body/eval_jaxpr/ppermute | solution.py:16
  121.9 8.8 %all-to-all-start.6 = ((bf16[4,128,128]{2,0,1:T(4,128)(2,1)}), bf16[4,128,128]{2,0,1:T(4,128)(2,1)S(1)}, u32[]{:S(2)}, u32[]{:S(2)}) async-start(bf16[4,128,128]{2,0,1:T(4,128)(2,1)} %copy.72), calls=%async_computation.6 | async-start | bytes 262144 | tf_op jit(solution)/shard_map/all_to_all | solution.py:187
  130.7 5.7 %all-to-all-start.7 = ((bf16[4,128,128]{2,0,1:T(4,128)(2,1)}), bf16[4,128,128]{2,0,1:T(4,128)(2,1)S(1)}, u32[]{:S(2)}, u32[]{:S(2)}) async-start(bf16[4,128,128]{2,0,1:T(4,128)(2,1)} %copy.71), calls=%async_computation.7 | async-start | bytes 262144 | tf_op jit(solution)/shard_map/all_to_all | solution.py:190
  136.4 4.3 %copy-start.3 = (bf16[4,4,128,128]{3,2,1,0:T(8,128)(2,1)S(1)}, bf16[4,4,128,128]{3,2,1,0:T(8,128)(2,1)}, u32[]{:S(2)}) copy-start(bf16[4,4,128,128]{3,2,1,0:T(8,128)(2,1)} %get-tuple-element.1399) | copy-start | bytes 1572868
  136.4 5.5 %all-to-all-start.5 = ((bf16[16,128,128]{2,0,1:T(8,128)(2,1)}), bf16[16,128,128]{2,0,1:T(8,128)(2,1)S(1)}, u32[]{:S(2)}, u32[]{:S(2)}) async-start(bf16[16,128,128]{2,0,1:T(8,128)(2,1)} %bitcast.59), calls=%async_computation.5 | async-start | bytes 1048576 | tf_op jit(solution)/shard_map/all_to_all | solution.py:180
  141.9 4.9 %all-to-all-start.3 = ((bf16[16,128,128]{2,0,1:T(8,128)(2,1)}), bf16[16,128,128]{2,0,1:T(8,128)(2,1)S(1)}, u32[]{:S(2)}, u32[]{:S(2)}) async-start(bf16[16,128,128]{2,0,1:T(8,128)(2,1)} %bitcast.48), calls=%async_computation.3 | async-start | bytes 1048576 | tf_op jit(solution)/shard_map/all_to_all | solution.py:107
where the time goes:
time: 149 us; the launch traced here: 148 us
  starting transfers between devices  67.3 us (45%)
  other arithmetic  24.2 us (16%)
  waiting for transfers between devices  20.7 us (14%)
  local copies, waits for them, and re-layouts  18.6 us (12%)
  matrix products  10.8 us (7%)
  loops' own time  3.92 us (3%)
  between operations  2.11 us (1%)
    ppermute x8, starting transfers between devices, shifted(): return lax.ppermute(block, axis, route)  33.7 us
    ppermute x8, waiting for transfers between devices, shifted(): return lax.ppermute(block, axis, route)  18.4 us
    all_to_all x1, starting transfers between devices, shards(): lax.all_to_all(key_total.astype(jnp.bfloat16), 'head', split_axis=1, conc...  7.67 us
    reduce_or x3, other arithmetic, backward_step(): jnp.any(visible)  4.99 us
    reduce_or x3, other arithmetic, forward_step(): return lax.cond(jnp.any(visible), attend, lambda carried: carried, online)  4.31 us
    all_to_all x1, starting transfers between devices, shards(): lax.all_to_all(query_matrix, 'head', split_axis=0, concat_axis=1, tiled=T...  4.16 us
    all_to_all x1, starting transfers between devices, shards(): lax.all_to_all(output_gradient, 'head', split_axis=0, concat_axis=1, tile...  3.83 us
    all_to_all x1, starting transfers between devices, shards(): lax.all_to_all(value_matrix, 'head', split_axis=0, concat_axis=1, tiled=T...  3.72 us
  transfers between devices with their start and end apart: 16, of which 8 were waited for; matrix products, arithmetic and copies ran while one was open for 11% of the time, Pallas kernels for 0%

commit v1 on v0

v1 whole, which is shorter than its diff:
```python
import jax
import jax.numpy as jnp
from jax import lax
from jax.experimental import pallas as pl
from jax.experimental.pallas import tpu as pltpu
from jax.sharding import PartitionSpec as P

MESH = pl.DeviceIdType.MESH
SEGMENT = 512
GROUPS = 8
PER_GROUP = 4
ROWS = 64
SLOTS = 5
WINDOW = ROWS * SLOTS
LANES = PER_GROUP * ROWS
WIDTH = 128
OWN = 4
AHEAD = 4
HIDDEN = -1e30
LOG2E = 1.4426950408889634


def kernel(
    q_hbm, k_hbm, v_hbm, g_hbm, span_hbm, off_hbm,
    attn_hbm, dq_hbm, dk_hbm, dv_hbm,
    qv, gv, kv, attn_v, dq_v, part, xs, xr, t2, ra, t1, rb, dkv, spans, offset,
    load_sem, hop1_s, hop1_r, hop2_s, hop2_r, pa_s, pa_r, pb_s, pb_r,
    x_s, x_r, a_s, a_r, b_s, b_r, out_sem, dkv_sem,
):
    core = lax.axis_index("head")
    here = lax.axis_index("seq")
    count = lax.axis_size("seq")
    after = {"seq": lax.rem(here + 1, count)}
    before = {"seq": lax.rem(here + count - 1, count)}
    partner = {"head": 1 - core}
    block = here * 2 + core
    scale = WIDTH ** -0.5

    barrier = pltpu.get_barrier_semaphore()
    for other in (after, before, partner):
        pl.semaphore_signal(barrier, inc=1, device_id=other, device_id_type=MESH)

    own_rows = pl.ds(OWN * ROWS, ROWS)
    loads = [
        pltpu.make_async_copy(k_hbm, kv.at[:, 0, own_rows, :], load_sem.at[0]),
        pltpu.make_async_copy(v_hbm, kv.at[:, 1, own_rows, :], load_sem.at[1]),
        pltpu.make_async_copy(q_hbm, qv, load_sem.at[2]),
        pltpu.make_async_copy(g_hbm, gv, load_sem.at[3]),
        pltpu.make_async_copy(span_hbm, spans, load_sem.at[4]),
        pltpu.make_async_copy(off_hbm, offset, load_sem.at[5]),
    ]
    for load in loads:
        load.start()
    xr[:, pl.ds(2 * core, 1)] = jnp.zeros((GROUPS, 1, 2, ROWS, WIDTH), jnp.bfloat16)

    def slot(g, s):
        return kv.at[g, :, pl.ds(pl.multiple_of(s * ROWS, ROWS), ROWS), :]

    def remote(src, dst, send, recv, other):
        return pltpu.make_async_remote_copy(
            src_ref=src, dst_ref=dst, send_sem=send, recv_sem=recv,
            device_id=other, device_id_type=MESH,
        )

    def hop1(g):
        return remote(slot(g, OWN), slot(g, 2), hop1_s.at[g], hop1_r.at[g], after)

    def hop2(g):
        return remote(slot(g, 2), slot(g, 0), hop2_s.at[g], hop2_r.at[g], after)

    def pair_near(g):
        return remote(slot(g, 4 - 2 * core), slot(g, 3), pa_s.at[g], pa_r.at[g], partner)

    def pair_far(g):
        return remote(slot(g, 2 - 2 * core), slot(g, 1), pb_s.at[g], pb_r.at[g], partner)

    def cross(g):
        return remote(xs.at[g], xr.at[g, pl.ds(core, 2)], x_s.at[g], x_r.at[g], partner)

    def cross_in(g):
        return remote(xs.at[g], xr.at[g, pl.ds(1 - core, 2)], x_s.at[g], x_r.at[g], partner)

    def chain2(g):
        return remote(t2.at[g], ra.at[g], a_s.at[g], a_r.at[g], before)

    def chain1(g):
        return remote(t1.at[g], rb.at[g], b_s.at[g], b_r.at[g], before)

    def heads(g):
        return pl.ds(pl.multiple_of(PER_GROUP * g, PER_GROUP), PER_GROUP)

    def attn_store(g):
        return pltpu.make_async_copy(attn_v.at[heads(g)], attn_hbm.at[heads(g)], out_sem.at[0, g])

    def dq_store(g):
        return pltpu.make_async_copy(dq_v.at[heads(g)], dq_hbm.at[heads(g)], out_sem.at[1, g])

    def dk_store(g):
        return pltpu.make_async_copy(dkv.at[g, 0], dk_hbm.at[g], dkv_sem.at[0, g])

    def dv_store(g):
        return pltpu.make_async_copy(dkv.at[g, 1], dv_hbm.at[g], dkv_sem.at[1, g])

    def on_hop1(g):
        hop1(g).wait_recv()
        hop2(g).start()

        @pl.when(g + AHEAD < GROUPS)
        def _():
            hop1(g + AHEAD).start()

        pair_near(g).start()

    def on_hop2(g):
        hop2(g).wait_recv()
        pair_far(g).start()

    lane = lax.broadcasted_iota(jnp.int32, (1, LANES), 1)
    row_in_block = lane & (ROWS - 1)
    query_row = row_in_block + OWN * ROWS

    def compute(g):
        pair_near(g).wait_recv()
        pair_far(g).wait_recv()
        span_of = [spans[PER_GROUP * g + a] for a in range(PER_GROUP)]
        span = jnp.where(
            lane < 2 * ROWS,
            jnp.where(lane < ROWS, span_of[0], span_of[1]),
            jnp.where(lane < 3 * ROWS, span_of[2], span_of[3]),
        )
        into_segment = (offset[0] + block * ROWS + row_in_block) & (SEGMENT - 1)
        lowest = query_row - jnp.minimum(span - 1, into_segment)
        lowest = jnp.maximum(lowest, (OWN - block) * ROWS)
        keys = kv[g, 0]
        values = kv[g, 1]
        queries = qv[heads(g)].reshape(LANES, WIDTH)
        grads = gv[heads(g)].reshape(LANES, WIDTH)
        last = (((1,), (1,)), ((), ()))
        first = (((0,), (0,)), ((), ()))
        scores = lax.dot_general(keys, queries, last, preferred_element_type=jnp.float32)
        prob_grad = lax.dot_general(values, grads, last, preferred_element_type=jnp.float32)
        key_row = lax.broadcasted_iota(jnp.int32, (WINDOW, LANES), 0)
        visible = (key_row >= lowest) & (key_row <= query_row)
        scores = jnp.where(visible, scores, HIDDEN)
        row_max = jnp.max(scores, axis=0, keepdims=True)
        weights = jnp.exp2((scores - row_max) * (scale * LOG2E))
        inverse = 1.0 / jnp.sum(weights, axis=0, keepdims=True)
        row_delta = jnp.sum(weights * prob_grad, axis=0, keepdims=True) * inverse
        attn = lax.dot_general(
            values, weights.astype(jnp.bfloat16), first, preferred_element_type=jnp.float32
        ) * inverse
        attn_v[heads(g)] = attn.T.astype(jnp.bfloat16).reshape(PER_GROUP, ROWS, WIDTH)
        attn_store(g).start()
        probs = (weights * inverse).astype(jnp.bfloat16)
        score_grad = (weights * ((prob_grad - row_delta) * (inverse * scale))).astype(jnp.bfloat16)
        dkey = jnp.dot(score_grad, queries, preferred_element_type=jnp.float32)
        dvalue = jnp.dot(probs, grads, preferred_element_type=jnp.float32)
        for j, s in enumerate((1, 3)):
            rows = slice(s * ROWS, (s + 1) * ROWS)
            xs[g, j, 0] = dkey[rows].astype(jnp.bfloat16)
            xs[g, j, 1] = dvalue[rows].astype(jnp.bfloat16)
        cross(g).start()
        for j, s in enumerate((0, 2, 4)):
            rows = slice(s * ROWS, (s + 1) * ROWS)
            part[g, j, 0] = dkey[rows]
            part[g, j, 1] = dvalue[rows]
        dquery = lax.dot_general(keys, score_grad, first, preferred_element_type=jnp.float32)
        dq_v[heads(g)] = dquery.T.astype(jnp.bfloat16).reshape(PER_GROUP, ROWS, WIDTH)
        dq_store(g).start()

    def on_cross(g):
        cross_in(g).wait_recv()
        t2[g] = (part[g, 0] + xr[g, 0].astype(jnp.float32)).astype(jnp.bfloat16)
        chain2(g).start()

    def on_chain2(g):
        chain2(g).wait_recv()
        total = part[g, 1] + xr[g, 1].astype(jnp.float32) + ra[g].astype(jnp.float32)
        t1[g] = total.astype(jnp.bfloat16)
        chain1(g).start()

    def on_chain1(g):
        chain1(g).wait_recv()
        total = part[g, 2] + xr[g, 2].astype(jnp.float32) + rb[g].astype(jnp.float32)
        dkv[g] = total.astype(jnp.bfloat16)
        dk_store(g).start()
        dv_store(g).start()

    loads[0].wait()
    loads[1].wait()
    pl.semaphore_wait(barrier, 3)
    for g in range(AHEAD):
        hop1(g).start()
    loads[2].wait()
    loads[3].wait()
    loads[4].wait()
    loads[5].wait()

    stages = ((on_hop1, 3), (on_hop2, 1), (compute, 0), (on_cross, -1), (on_chain2, -3), (on_chain1, -5))

    def turn(t, carry):
        for stage, lead in stages:
            g = t + lead

            @pl.when((g >= 0) & (g < GROUPS))
            def _(stage=stage, g=g):
                stage(g)

        return carry

    lax.fori_loop(-3, GROUPS + 5, turn, 0)

    def finish(g, carry):
        hop1(g).wait_send()
        hop2(g).wait_send()
        pair_near(g).wait_send()
        pair_far(g).wait_send()
        cross(g).wait_send()
        chain2(g).wait_send()
        chain1(g).wait_send()
        attn_store(g).wait()
        dq_store(g).wait()
        dk_store(g).wait()
        dv_store(g).wait()
        return carry

    lax.fori_loop(0, GROUPS, finish, 0)


def shards(query_matrix, key_matrix, value_matrix, output_gradient, query_head_spans, slab_offset):
    any_space = pl.BlockSpec(memory_space=pl.ANY)
    half = jnp.bfloat16
    group_sems = pltpu.SemaphoreType.DMA((GROUPS,))
    shapes = [
        jax.ShapeDtypeStruct(a.shape, a.dtype)
        for a in (query_matrix, query_matrix, key_matrix, value_matrix)
    ]
    return pl.pallas_call(
        kernel,
        out_shape=shapes,
        in_specs=[any_space] * 6,
        out_specs=[any_space] * 4,
        scratch_shapes=[
            pltpu.VMEM(query_matrix.shape, half),
            pltpu.VMEM(query_matrix.shape, half),
            pltpu.VMEM((GROUPS, 2, WINDOW, WIDTH), half),
            pltpu.VMEM(query_matrix.shape, half),
            pltpu.VMEM(query_matrix.shape, half),
            pltpu.VMEM((GROUPS, 3, 2, ROWS, WIDTH), jnp.float32),
            pltpu.VMEM((GROUPS, 2, 2, ROWS, WIDTH), half),
            pltpu.VMEM((GROUPS, 3, 2, ROWS, WIDTH), half),
            pltpu.VMEM((GROUPS, 2, ROWS, WIDTH), half),
            pltpu.VMEM((GROUPS, 2, ROWS, WIDTH), half),
            pltpu.VMEM((GROUPS, 2, ROWS, WIDTH), half),
            pltpu.VMEM((GROUPS, 2, ROWS, WIDTH), half),
            pltpu.VMEM((GROUPS, 2, ROWS, WIDTH), half),
            pltpu.SMEM((GROUPS * PER_GROUP,), jnp.int32),
            pltpu.SMEM((1,), jnp.int32),
            pltpu.SemaphoreType.DMA((6,)),
        ]
        + [group_sems] * 14
        + [pltpu.SemaphoreType.DMA((2, GROUPS))] * 2,
        compiler_params=pltpu.CompilerParams(collective_id=0, has_side_effects=True),
    )(query_matrix, key_matrix, value_matrix, output_gradient, query_head_spans, slab_offset)


def solution(mesh):
    blocks = P(None, ("seq", "head"), None)
    return jax.shard_map(
        shards,
        mesh=mesh,
        in_specs=(blocks, blocks, blocks, blocks, P(), P()),
        out_specs=(blocks, blocks, blocks, blocks),
        check_vma=False,
    )
```

time: 149 us -> 51 us (0.34)
  the two profiles are of different devices: /device:TPU:255 before, /device:TPU:1 now
where the time goes in v1:
time: 51 us; the launch traced here: 50.8 us
  Pallas kernels  45 us (88%)
  local copies, waits for them, and re-layouts  4.56 us (9%)
  between operations  1.3 us (3%)
    pallas_call x1, Pallas kernels, shards(): pl.pallas_call(kernel, out_shape=shapes, in_specs=[any_space] * 6, out_sp...  45 us
    unnamed x10, local copies, waits for them, and re-layouts  4.56 us

profile of v1, /device:TPU:1, one launch (start us, length us, event | category | flops | bytes accessed | tf_op | source)
XLA Modules:
  0.0 50.8 jit_solution(6267561664697021938)
XLA Ops:
  1.3 45.0 %shard_map.93 = (bf16[32,64,128]{2,1,0:T(8,128)(2,1)}, bf16[32,64,128]{2,1,0:T(8,128)(2,1)}, bf16[8,64,128]{2,1,0:T(8,128)(2,1)}, bf16[8,64,128]{2,1,0:T(8,128)(2,1)}) custom-call(bf16[32,64,128]{2,1,0:T(8,128)(2,1)} %q_hbm.1, bf16[8,64,128]{2,1,0:T(8,128)(2,1)} %k_hbm.1, bf16[8,64,128]{2,1,0:T(8,128)(2,1)} %v_hbm.1, bf16[32,64,128]{2,1,0:T(8,128)(2,1)} %g_hbm.1, ...), custom_call_target="tpu_custom_call" | custom-call | tf_op jit(solution)/shard_map/pallas_call | solution.py:238
  46.2 0.0 copy-start
  46.3 1.9 %copy.15 = bf16[32,64,128]{2,1,0:T(8,128)(2,1)} copy(bf16[32,64,128]{2,1,0:T(8,128)(2,1)} %get-tuple-element.8) | data formatting | bytes 1048576
  48.2 0.0 copy-done
  48.2 0.0 copy-start.2
  48.2 0.8 %copy.16 = bf16[32,64,128]{2,1,0:T(8,128)(2,1)} copy(bf16[32,64,128]{2,1,0:T(8,128)(2,1)S(1)} %copy-done) | data formatting | bytes 1048576
  49.0 0.2 copy-done.2
  49.2 0.0 copy-start.1
  49.2 0.7 %copy.17 = bf16[8,64,128]{2,1,0:T(8,128)(2,1)} copy(bf16[8,64,128]{2,1,0:T(8,128)(2,1)S(1)} %copy-done.2) | data formatting | bytes 262144
  49.9 0.3 copy-done.1
  50.2 0.7 %copy.18 = bf16[8,64,128]{2,1,0:T(8,128)(2,1)} copy(bf16[8,64,128]{2,1,0:T(8,128)(2,1)S(1)} %copy-done.1) | data formatting | bytes 262144
Async XLA Ops:
  46.2 1.9 %copy-start = (bf16[32,64,128]{2,1,0:T(8,128)(2,1)S(1)}, bf16[32,64,128]{2,1,0:T(8,128)(2,1)}, u32[]{:S(2)}) copy-start(bf16[32,64,128]{2,1,0:T(8,128)(2,1)} %get-tuple-element.9) | copy-start | bytes 1572868
  48.2 1.0 %copy-start.2 = (bf16[8,64,128]{2,1,0:T(8,128)(2,1)S(1)}, bf16[8,64,128]{2,1,0:T(8,128)(2,1)}, u32[]{:S(2)}) copy-start(bf16[8,64,128]{2,1,0:T(8,128)(2,1)} %get-tuple-element.10) | copy-start | bytes 393220
  49.2 1.0 %copy-start.1 = (bf16[8,64,128]{2,1,0:T(8,128)(2,1)S(1)}, bf16[8,64,128]{2,1,0:T(8,128)(2,1)}, u32[]{:S(2)}) copy-start(bf16[8,64,128]{2,1,0:T(8,128)(2,1)} %get-tuple-element.11) | copy-start | bytes 393220

commit v2 on v1

--- a/solution.py
+++ b/solution.py
@@ -15,30 +15,46 @@
 LANES = PER_GROUP * ROWS
 WIDTH = 128
 OWN = 4
-AHEAD = 4
+AHEAD = 8
+DIRECT_KEYS = 8
+DIRECT_GRADS = 8
+LEADS = (3, 1, -1, -2, -4)
 HIDDEN = -1e30
 LOG2E = 1.4426950408889634
 
 
 def kernel(
     q_hbm, k_hbm, v_hbm, g_hbm, span_hbm, off_hbm,
-    attn_hbm, dq_hbm, dk_hbm, dv_hbm,
-    qv, gv, kv, attn_v, dq_v, part, xs, xr, t2, ra, t1, rb, dkv, spans, offset,
+    attn_v, dq_v, dk_v, dv_v,
+    qv, gv, kv, part, xs, xr, t2, ra, t1, rb, spans, offset,
     load_sem, hop1_s, hop1_r, hop2_s, hop2_r, pa_s, pa_r, pb_s, pb_r,
-    x_s, x_r, a_s, a_r, b_s, b_r, out_sem, dkv_sem,
+    x_s, x_r, a_s, a_r, b_s, b_r,
 ):
     core = lax.axis_index("head")
     here = lax.axis_index("seq")
     count = lax.axis_size("seq")
     after = {"seq": lax.rem(here + 1, count)}
     before = {"seq": lax.rem(here + count - 1, count)}
+    after2 = {"seq": lax.rem(here + 2, count)}
+    before2 = {"seq": lax.rem(here + count - 2, count)}
     partner = {"head": 1 - core}
     block = here * 2 + core
     scale = WIDTH ** -0.5
 
     barrier = pltpu.get_barrier_semaphore()
-    for other in (after, before, partner):
+    has_before = here >= 1
+    has_after = here < count - 1
+    two_before = here >= 2
+    two_after = here < count - 2
+
+    def greet(other):
         pl.semaphore_signal(barrier, inc=1, device_id=other, device_id_type=MESH)
+
+    greet(partner)
+    pl.when(has_before)(lambda: greet(before))
+    pl.when(has_after)(lambda: greet(after))
+    pl.when(two_before)(lambda: greet(before2))
+    pl.when(two_after)(lambda: greet(after2))
 
     own_rows = pl.ds(OWN * ROWS, ROWS)
     loads = [
@@ -51,6 +67,17 @@
     ]
     for load in loads:
         load.start()
+
+    def clear(ref):
+        ref[...] = jnp.zeros(ref.shape, ref.dtype)
+
+    pl.when(jnp.logical_not(two_before))(lambda: clear(kv.at[:, :, pl.ds(0, ROWS), :]))
+    pl.when(jnp.logical_not(has_before))(lambda: clear(kv.at[:, :, pl.ds(2 * ROWS, ROWS), :]))
+    pl.when(jnp.logical_not(has_after))(lambda: clear(ra))
+    if DIRECT_GRADS:
+        direct_part = ra.at[pl.ds(GROUPS - DIRECT_GRADS, DIRECT_GRADS)]
+        pl.when(has_after & jnp.logical_not(two_after))(lambda: clear(direct_part))
+    pl.when(jnp.logical_not(has_after))(lambda: clear(rb))
     xr[:, pl.ds(2 * core, 1)] = jnp.zeros((GROUPS, 1, 2, ROWS, WIDTH), jnp.bfloat16)
 
     def slot(g, s):
@@ -68,6 +95,9 @@
     def hop2(g):
         return remote(slot(g, 2), slot(g, 0), hop2_s.at[g], hop2_r.at[g], after)
 
+    def hop2_direct(g):
+        return remote(slot(g, OWN), slot(g, 0), hop2_s.at[g], hop2_r.at[g], after2)
+
     def pair_near(g):
         return remote(slot(g, 4 - 2 * core), slot(g, 3), pa_s.at[g], pa_r.at[g], partner)
 
@@ -83,36 +113,29 @@
     def chain2(g):
         return remote(t2.at[g], ra.at[g], a_s.at[g], a_r.at[g], before)
 
+    def chain2_direct(g):
+        return remote(t2.at[g], ra.at[g], a_s.at[g], a_r.at[g], before2)
+
     def chain1(g):
         return remote(t1.at[g], rb.at[g], b_s.at[g], b_r.at[g], before)
 
     def heads(g):
         return pl.ds(pl.multiple_of(PER_GROUP * g, PER_GROUP), PER_GROUP)
 
-    def attn_store(g):
-        return pltpu.make_async_copy(attn_v.at[heads(g)], attn_hbm.at[heads(g)], out_sem.at[0, g])
-
-    def dq_store(g):
-        return pltpu.make_async_copy(dq_v.at[heads(g)], dq_hbm.at[heads(g)], out_sem.at[1, g])
-
-    def dk_store(g):
-        return pltpu.make_async_copy(dkv.at[g, 0], dk_hbm.at[g], dkv_sem.at[0, g])
-
-    def dv_store(g):
-        return pltpu.make_async_copy(dkv.at[g, 1], dv_hbm.at[g], dkv_sem.at[1, g])
-
     def on_hop1(g):
-        hop1(g).wait_recv()
-        hop2(g).start()
-
-        @pl.when(g + AHEAD < GROUPS)
+        @pl.when(has_before)
+        def _():
+            hop1(g).wait_recv()
+            pl.when(has_after & (g >= DIRECT_KEYS))(lambda: hop2(g).start())
+
+        @pl.when(has_after & (g + AHEAD < GROUPS))
         def _():
             hop1(g + AHEAD).start()
 
         pair_near(g).start()
 
     def on_hop2(g):
-        hop2(g).wait_recv()
+        pl.when(two_before)(lambda: hop2(g).wait_recv())
         pair_far(g).start()
 
     lane = lax.broadcasted_iota(jnp.int32, (1, LANES), 1)
@@ -150,7 +173,6 @@
             values, weights.astype(jnp.bfloat16), first, preferred_element_type=jnp.float32
         ) * inverse
         attn_v[heads(g)] = attn.T.astype(jnp.bfloat16).reshape(PER_GROUP, ROWS, WIDTH)
-        attn_store(g).start()
         probs = (weights * inverse).astype(jnp.bfloat16)
         score_grad = (weights * ((prob_grad - row_delta) * (inverse * scale))).astype(jnp.bfloat16)
         dkey = jnp.dot(score_grad, queries, preferred_element_type=jnp.float32)
@@ -166,37 +188,57 @@
             part[g, j, 1] = dvalue[rows]
         dquery = lax.dot_general(keys, score_grad, first, preferred_element_type=jnp.float32)
         dq_v[heads(g)] = dquery.T.astype(jnp.bfloat16).reshape(PER_GROUP, ROWS, WIDTH)
-        dq_store(g).start()
+
+    def send_t1(g, total):
+        t1[g] = total.astype(jnp.bfloat16)
+        chain1(g).start()
 
     def on_cross(g):
         cross_in(g).wait_recv()
-        t2[g] = (part[g, 0] + xr[g, 0].astype(jnp.float32)).astype(jnp.bfloat16)
-        chain2(g).start()
+        direct = g >= GROUPS - DIRECT_GRADS
+
+        @pl.when(two_before)
+        def _():
+            t2[g] = (part[g, 0] + xr[g, 0].astype(jnp.float32)).astype(jnp.bfloat16)
+            pl.when(direct)(lambda: chain2_direct(g).start())
+            pl.when(jnp.logical_not(direct))(lambda: chain2(g).start())
+
+        @pl.when(has_before & direct)
+        def _():
+            send_t1(g, part[g, 1] + xr[g, 1].astype(jnp.float32))
 
     def on_chain2(g):
-        chain2(g).wait_recv()
-        total = part[g, 1] + xr[g, 1].astype(jnp.float32) + ra[g].astype(jnp.float32)
-        t1[g] = total.astype(jnp.bfloat16)
-        chain1(g).start()
+        @pl.when(has_before & (g < GROUPS - DIRECT_GRADS))
+        def _():
+            pl.when(has_after)(lambda: chain2(g).wait_recv())
+            send_t1(g, part[g, 1] + xr[g, 1].astype(jnp.float32) + ra[g].astype(jnp.float32))
 
     def on_chain1(g):
-        chain1(g).wait_recv()
+        direct = g >= GROUPS - DIRECT_GRADS
+        pl.when(has_after)(lambda: chain1(g).wait_recv())
+        pl.when(two_after & direct)(lambda: chain2_direct(g).wait_recv())
         total = part[g, 2] + xr[g, 2].astype(jnp.float32) + rb[g].astype(jnp.float32)
-        dkv[g] = total.astype(jnp.bfloat16)
-        dk_store(g).start()
-        dv_store(g).start()
+        extra = ra[g].astype(jnp.float32)
+        total = total + jnp.where(direct, extra, jnp.zeros_like(extra))
+        dk_v[g] = total[0].astype(jnp.bfloat16)
+        dv_v[g] = total[1].astype(jnp.bfloat16)
 
     loads[0].wait()
     loads[1].wait()
-    pl.semaphore_wait(barrier, 3)
+    pl.semaphore_wait(barrier, 1 + jnp.minimum(here, 2) + jnp.minimum(count - 1 - here, 2))
+
     for g in range(AHEAD):
-        hop1(g).start()
+        pl.when(has_after)(lambda g=g: hop1(g).start())
+        if g < DIRECT_KEYS:
+            pl.when(two_after)(lambda g=g: hop2_direct(g).start())
+
     loads[2].wait()
     loads[3].wait()
     loads[4].wait()
     loads[5].wait()
 
-    stages = ((on_hop1, 3), (on_hop2, 1), (compute, 0), (on_cross, -1), (on_chain2, -3), (on_chain1, -5))
+    works = (on_hop1, on_hop2, compute, on_cross, on_chain2, on_chain1)
+    stages = tuple(zip(works, LEADS[:2] + (0,) + LEADS[2:]))
 
     def turn(t, carry):
         for stage, lead in stages:
@@ -208,48 +250,55 @@
 
         return carry
 
-    lax.fori_loop(-3, GROUPS + 5, turn, 0)
+    lax.fori_loop(-LEADS[0], GROUPS - LEADS[-1], turn, 0)
 
     def finish(g, carry):
-        hop1(g).wait_send()
-        hop2(g).wait_send()
+        pl.when(has_after)(lambda: hop1(g).wait_send())
+        relayed = g >= DIRECT_KEYS
+        pl.when((relayed & has_before & has_after) | (jnp.logical_not(relayed) & two_after))(
+            lambda: hop2(g).wait_send()
+        )
         pair_near(g).wait_send()
         pair_far(g).wait_send()
         cross(g).wait_send()
-        chain2(g).wait_send()
-        chain1(g).wait_send()
-        attn_store(g).wait()
-        dq_store(g).wait()
-        dk_store(g).wait()
-        dv_store(g).wait()
+        pl.when(two_before)(lambda: chain2(g).wait_send())
+        pl.when(has_before)(lambda: chain1(g).wait_send())
         return carry
 
     lax.fori_loop(0, GROUPS, finish, 0)
+
+
+def flush(*refs):
+    copies = [
+        pltpu.make_async_copy(refs[i], refs[4 + i], refs[8].at[i]) for i in range(4)
+    ]
+    for copy in copies:
+        copy.start()
+    for copy in copies:
+        copy.wait()
 
 
 def shards(query_matrix, key_matrix, value_matrix, output_gradient, query_head_spans, slab_offset):
     any_space = pl.BlockSpec(memory_space=pl.ANY)
+    vmem_space = pl.BlockSpec(memory_space=pltpu.VMEM)
     half = jnp.bfloat16
     group_sems = pltpu.SemaphoreType.DMA((GROUPS,))
     shapes = [
         jax.ShapeDtypeStruct(a.shape, a.dtype)
         for a in (query_matrix, query_matrix, key_matrix, value_matrix)
     ]
-    return pl.pallas_call(
+    results = pl.pallas_call(
         kernel,
-        out_shape=shapes,
+        out_shape=[pltpu.VMEM(a.shape, a.dtype) for a in shapes],
         in_specs=[any_space] * 6,
-        out_specs=[any_space] * 4,
+        out_specs=[vmem_space] * 4,
         scratch_shapes=[
             pltpu.VMEM(query_matrix.shape, half),
             pltpu.VMEM(query_matrix.shape, half),
             pltpu.VMEM((GROUPS, 2, WINDOW, WIDTH), half),
-            pltpu.VMEM(query_matrix.shape, half),
-            pltpu.VMEM(query_matrix.shape, half),
             pltpu.VMEM((GROUPS, 3, 2, ROWS, WIDTH), jnp.float32),
             pltpu.VMEM((GROUPS, 2, 2, ROWS, WIDTH), half),
             pltpu.VMEM((GROUPS, 3, 2, ROWS, WIDTH), half),
-            pltpu.VMEM((GROUPS, 2, ROWS, WIDTH), half),
             pltpu.VMEM((GROUPS, 2, ROWS, WIDTH), half),
             pltpu.VMEM((GROUPS, 2, ROWS, WIDTH), half),
             pltpu.VMEM((GROUPS, 2, ROWS, WIDTH), half),
@@ -258,10 +307,16 @@
             pltpu.SMEM((1,), jnp.int32),
             pltpu.SemaphoreType.DMA((6,)),
         ]
-        + [group_sems] * 14
-        + [pltpu.SemaphoreType.DMA((2, GROUPS))] * 2,
+        + [group_sems] * 14,
         compiler_params=pltpu.CompilerParams(collective_id=0, has_side_effects=True),
     )(query_matrix, key_matrix, value_matrix, output_gradient, query_head_spans, slab_offset)
+    return pl.pallas_call(
+        flush,
+        out_shape=shapes,
+        in_specs=[vmem_space] * 4,
+        out_specs=[any_space] * 4,
+        scratch_shapes=[pltpu.SemaphoreType.DMA((4,))],
+    )(*[pltpu.with_memory_space_constraint(r, pltpu.VMEM) for r in results])
 
 
 def solution(mesh):

time: 51 us -> 38.1 us (0.75)
  the two profiles are of different devices: /device:TPU:1 before, /device:TPU:255 now
where the time goes in v2:
time: 38.1 us; the launch traced here: 37.5 us
  Pallas kernels  36.3 us (95%)
  between operations  1.29 us (3%)
    pallas_call x1, Pallas kernels, shards(): pl.pallas_call(kernel, out_shape=[pltpu.VMEM(a.shape, a.dtype) for a in s...  35.2 us
    pallas_call x1, Pallas kernels, shards(): pl.pallas_call(flush, out_shape=shapes, in_specs=[vmem_space] * 4, out_sp...  1.08 us

profile of v2, /device:TPU:255, one launch (start us, length us, event | category | flops | bytes accessed | tf_op | source)
XLA Modules:
  0.0 37.5 jit_solution(10706266637865574501)
XLA Ops:
  1.3 35.2 %shard_map.93 = (bf16[32,64,128]{2,1,0:T(8,128)(2,1)S(1)}, bf16[32,64,128]{2,1,0:T(8,128)(2,1)S(1)}, bf16[8,64,128]{2,1,0:T(8,128)(2,1)S(1)}, bf16[8,64,128]{2,1,0:T(8,128)(2,1)S(1)}) custom-call(bf16[32,64,128]{2,1,0:T(8,128)(2,1)} %q_hbm.1, bf16[8,64,128]{2,1,0:T(8,128)(2,1)} %k_hbm.1, bf16[8,64,128]{2,1,0:T(8,128)(2,1)} %v_hbm.1, ...), custom_call_target="tpu_custom_call" | custom-call | tf_op jit(solution)/shard_map/pallas_call | solution.py:290
  36.5 1.1 %shard_map.94 = (bf16[32,64,128]{2,1,0:T(8,128)(2,1)}, bf16[32,64,128]{2,1,0:T(8,128)(2,1)}, bf16[8,64,128]{2,1,0:T(8,128)(2,1)}, bf16[8,64,128]{2,1,0:T(8,128)(2,1)}) custom-call(bf16[32,64,128]{2,1,0:T(8,128)(2,1)S(1)} %get-tuple-element.8.refs_0_, bf16[32,64,128]{2,1,0:T(8,128)(2,1)S(1)} %get-tuple-element.9.refs_1_, ...), custom_call_target="tpu_custom_call" | custom-call | tf_op jit(solution)/shard_map/pallas_call | solution.py:313

commit v3 on v2

--- a/solution.py
+++ b/solution.py
@@ -18,7 +18,7 @@
 AHEAD = 8
 DIRECT_KEYS = 8
 DIRECT_GRADS = 8
-LEADS = (3, 1, -1, -2, -4)
+LEADS = (1, 1, -1, -2, -8)
 HIDDEN = -1e30
 LOG2E = 1.4426950408889634
 
@@ -169,10 +169,6 @@
         weights = jnp.exp2((scores - row_max) * (scale * LOG2E))
         inverse = 1.0 / jnp.sum(weights, axis=0, keepdims=True)
         row_delta = jnp.sum(weights * prob_grad, axis=0, keepdims=True) * inverse
-        attn = lax.dot_general(
-            values, weights.astype(jnp.bfloat16), first, preferred_element_type=jnp.float32
-        ) * inverse
-        attn_v[heads(g)] = attn.T.astype(jnp.bfloat16).reshape(PER_GROUP, ROWS, WIDTH)
         probs = (weights * inverse).astype(jnp.bfloat16)
         score_grad = (weights * ((prob_grad - row_delta) * (inverse * scale))).astype(jnp.bfloat16)
         dkey = jnp.dot(score_grad, queries, preferred_element_type=jnp.float32)
@@ -186,6 +182,10 @@
             rows = slice(s * ROWS, (s + 1) * ROWS)
             part[g, j, 0] = dkey[rows]
             part[g, j, 1] = dvalue[rows]
+        attn = lax.dot_general(
+            values, weights.astype(jnp.bfloat16), first, preferred_element_type=jnp.float32
+        ) * inverse
+        attn_v[heads(g)] = attn.T.astype(jnp.bfloat16).reshape(PER_GROUP, ROWS, WIDTH)
         dquery = lax.dot_general(keys, score_grad, first, preferred_element_type=jnp.float32)
         dq_v[heads(g)] = dquery.T.astype(jnp.bfloat16).reshape(PER_GROUP, ROWS, WIDTH)
 

time: 38.1 us -> 35.5 us (0.932)
  Pallas kernels: 36.3 us -> 34 us
    pallas_call x1, Pallas kernels: 35.2 us -> 32.9 us  [shards(): pl.pallas_call(kernel, out_shape=[pltpu.VMEM(a.shape, a.dtype) for a in s...]
where the time goes in v3:
time: 35.5 us; the launch traced here: 35.3 us
  Pallas kernels  34 us (96%)
  between operations  1.29 us (4%)
    pallas_call x1, Pallas kernels, shards(): pl.pallas_call(kernel, out_shape=[pltpu.VMEM(a.shape, a.dtype) for a in s...  32.9 us
    pallas_call x1, Pallas kernels, shards(): pl.pallas_call(flush, out_shape=shapes, in_specs=[vmem_space] * 4, out_sp...  1.08 us

profile of v3, /device:TPU:255, one launch (start us, length us, event | category | flops | bytes accessed | tf_op | source)
XLA Modules:
  0.0 35.3 jit_solution(2366840250889036911)
XLA Ops:
  1.3 32.9 %shard_map.93 = (bf16[32,64,128]{2,1,0:T(8,128)(2,1)S(1)}, bf16[32,64,128]{2,1,0:T(8,128)(2,1)S(1)}, bf16[8,64,128]{2,1,0:T(8,128)(2,1)S(1)}, bf16[8,64,128]{2,1,0:T(8,128)(2,1)S(1)}) custom-call(bf16[32,64,128]{2,1,0:T(8,128)(2,1)} %q_hbm.1, bf16[8,64,128]{2,1,0:T(8,128)(2,1)} %k_hbm.1, bf16[8,64,128]{2,1,0:T(8,128)(2,1)} %v_hbm.1, ...), custom_call_target="tpu_custom_call" | custom-call | tf_op jit(solution)/shard_map/pallas_call | solution.py:290
  34.2 1.1 %shard_map.94 = (bf16[32,64,128]{2,1,0:T(8,128)(2,1)}, bf16[32,64,128]{2,1,0:T(8,128)(2,1)}, bf16[8,64,128]{2,1,0:T(8,128)(2,1)}, bf16[8,64,128]{2,1,0:T(8,128)(2,1)}) custom-call(bf16[32,64,128]{2,1,0:T(8,128)(2,1)S(1)} %get-tuple-element.8.refs_0_, bf16[32,64,128]{2,1,0:T(8,128)(2,1)S(1)} %get-tuple-element.9.refs_1_, ...), custom_call_target="tpu_custom_call" | custom-call | tf_op jit(solution)/shard_map/pallas_call | solution.py:313
